TPU v7x, 256 devices: a whole 4x4x8 slice. The times are simulated.
256 devices in a mesh: req: 32 (over z_hi, x, y), tp: 8 (over z_lo, core).
Axes of the slice: x: 4, y: 4, z: 8 (z_hi: 2, z_lo: 4; z = z_hi * 4 + z_lo), core: 2. Of those that a mesh axis runs over, the one named last changes fastest.
Arguments:
- hidden: bfloat16 [4096, 2048], P('req', 'tp'), may hold values from -6 to 6
- attn_gain: bfloat16 [2048], replicated, may hold values from 0.099609375 to 1.8984375
- w_qkv: bfloat16 [3, 2048, 2048], P(None, None, 'tp'), may hold values from -0.125 to 0.125
- w_out: bfloat16 [2048, 2048], P('tp'), may hold values from -0.125 to 0.125
- kv_cache: bfloat16 [2, 32, 1024, 2048], P(None, 'req', None, 'tp'), as said below
- holder_slot: int32 [32], replicated, may hold values from 0 to 31, as said below
- lengths: int32 [32], P('req'), may hold values from 1 to 1024, as said below
- ffn_gain: bfloat16 [2048], replicated, may hold values from 0.099609375 to 1.8984375
- w_router: bfloat16 [2048, 32], replicated
- expert_ids: int32 [4096, 6], P('req'), may hold values from 0 to 31, all different within a row; in each aligned block of 128 rows (0 to 127, 128 to 255, ...) at most 32 rows name the same one
- w_exp_in: bfloat16 [32, 2, 2048, 1408], P('req', None, None, 'tp'), may hold values from -0.4375 to 0.4375
- w_exp_down: bfloat16 [32, 1408, 2048], P('req', 'tp'), may hold values from -0.5 to 0.5
- w_sh_in: bfloat16 [2, 2048, 1408], P(None, None, 'tp'), may hold values from -0.125 to 0.125
- w_sh_down: bfloat16 [1408, 2048], P('tp'), may hold values from -0.15625 to 0.15625
- final_gain: bfloat16 [2048], replicated, may hold values from 0.5 to 1.5
- w_head: bfloat16 [51200, 2048], P(('req', 'tp')), may hold values from -0.5 to 0.5
Outputs:
- out_hidden: bfloat16 [4096, 2048], P('req', 'tp')
- new_cache: bfloat16 [2, 32, 128, 2048], P(None, 'req', None, 'tp')
- last_rms: float32 [32], replicated
- top_logit: float32 [32], replicated
Inputs may be any that keep to these rules, and one draw needn't show every extreme that they name: `kv_cache`: the cache in slot s lies on index s // 1 of req; request r is owned by index r. `holder_slot`: A permutation of the cache slots; about half of the requests keep their own slot. `lengths`: some request has exactly 1024 cached positions. `expert_ids`: within the rows of one device (128 aligned tokens) each expert is named by at most 32 rows, a bound that is reached.
All inputs are finite; a program needn't handle non-finite values.
Results may differ from a plain program's by a relative error of at most 0.025.
Values may be sent and summed in bfloat16 or wider, within the bound.
No kernel may reach another device: no remote copies, remote signals or barrier semaphores. Data moves between devices by JAX's collectives and lax.ppermute only.
A program may use at most 64 MiB of HBM per device.

v0:
```python
import jax
import jax.numpy as jnp
from jax import lax
from jax.sharding import PartitionSpec as P

HD = 128
TOPK = 6
CAP = 32
epsilon = 1e-06


def rms_scale(values, gain):
    return (
        values
        * lax.rsqrt(jnp.mean(values * values, axis=-1, keepdims=True) + epsilon)
        * gain.astype(jnp.float32)
    )


def rotate_half(values, positions):
    half_len = values.shape[-1] // 2
    freqs = 10000.0 ** (-2.0 * jnp.arange(half_len, dtype=jnp.float32) / values.shape[-1])
    angles = positions[..., None] * freqs
    cosine = jnp.cos(angles)[..., None, :]
    sine = jnp.sin(angles)[..., None, :]
    lead_half = values[..., :half_len]
    tail_half = values[..., half_len:]
    return jnp.concatenate(
        [lead_half * cosine - tail_half * sine, tail_half * cosine + lead_half * sine], axis=-1
    )


def attend(queries, keys_new, values_new, old_keys, old_values, lengths):
    context_len = old_keys.shape[1]
    new_len = queries.shape[1]
    all_keys = jnp.concatenate([old_keys, keys_new], axis=1)
    all_values = jnp.concatenate([old_values, values_new], axis=1)
    scores = jnp.einsum(
        "rthd,rshd->rhts", queries, all_keys, preferred_element_type=jnp.float32
    ) * queries.shape[-1] ** (-0.5)
    column = jnp.arange(context_len + new_len)[None, None, :]
    row_pos = jnp.arange(new_len)[None, :, None]
    visible = jnp.where(
        column < context_len, column < lengths[:, None, None], column - context_len <= row_pos
    )
    visible = visible[:, None]
    masked = jnp.where(visible, scores, -1e30)
    peak = jnp.max(masked, axis=-1, keepdims=True)
    raised = jnp.where(visible, jnp.exp(masked - peak), 0.0)
    weights = (raised / jnp.sum(raised, axis=-1, keepdims=True)).astype(jnp.bfloat16)
    mixed = jnp.einsum("rhts,rshd->rthd", weights, all_values, preferred_element_type=jnp.float32)
    return mixed.astype(jnp.bfloat16)


def expert_block(arrived, w_exp_in, w_exp_down):
    both = jnp.einsum("nekd,ecdf->cnekf", arrived, w_exp_in, preferred_element_type=jnp.float32)
    inner = (jax.nn.silu(both[0]) * both[1]).astype(jnp.bfloat16)
    return jnp.einsum(
        "nekf,efd->nekd", inner, w_exp_down, preferred_element_type=jnp.float32
    ).astype(jnp.bfloat16)


def local(
    hidden,
    attn_gain,
    w_qkv,
    w_out,
    kv_cache,
    holder_slot,
    lengths,
    ffn_gain,
    w_router,
    expert_ids,
    w_exp_in,
    w_exp_down,
    w_sh_in,
    w_sh_down,
    final_gain,
    w_head,
):
    req_size = lax.axis_size("req")
    tp_pos = lax.axis_index("tp")
    full_in = lax.all_gather(hidden, "tp", axis=1, tiled=True)
    tok_rows = full_in.shape[0]
    slot_count = kv_cache.shape[1]
    new_len = tok_rows // slot_count
    local_feat = hidden.shape[1]
    local_heads = w_qkv.shape[2] // HD
    normed = rms_scale(full_in.astype(jnp.float32), attn_gain).astype(jnp.bfloat16)
    projected = jnp.einsum("td,cde->cte", normed, w_qkv, preferred_element_type=jnp.float32)
    positions = (lengths[:, None] + jnp.arange(new_len, dtype=jnp.int32)[None, :]).astype(
        jnp.float32
    )
    shaped = projected.reshape(3, slot_count, new_len, local_heads, HD)
    queries = rotate_half(shaped[0], positions).astype(jnp.bfloat16)
    keys_new = rotate_half(shaped[1], positions).astype(jnp.bfloat16)
    values_new = shaped[2].astype(jnp.bfloat16)
    new_cache = jnp.stack([keys_new, values_new]).reshape(2, slot_count, new_len, local_heads * HD)
    spread = lax.all_to_all(kv_cache, "req", split_axis=2, concat_axis=1, tiled=True)
    ordered = jnp.take(spread, holder_slot, axis=1)
    fetched = lax.all_to_all(ordered, "req", split_axis=1, concat_axis=2, tiled=True)
    context_len = fetched.shape[2]
    old_pair = fetched.reshape(2, slot_count, context_len, local_heads, HD)
    attn_out = attend(queries, keys_new, values_new, old_pair[0], old_pair[1], lengths)
    attn_out = attn_out.reshape(tok_rows, local_heads * HD)
    attn_total = lax.psum(
        jnp.dot(attn_out, w_out, preferred_element_type=jnp.float32).astype(jnp.bfloat16), "tp"
    ).astype(jnp.float32)
    resid = (full_in.astype(jnp.float32) + attn_total).astype(jnp.bfloat16)
    ffn_in = rms_scale(resid.astype(jnp.float32), ffn_gain).astype(jnp.bfloat16)
    probs = jax.nn.softmax(jnp.dot(ffn_in, w_router, preferred_element_type=jnp.float32), axis=-1)
    experts_all = w_router.shape[1]
    expert_local = w_exp_in.shape[0]
    expert_iota = jnp.arange(experts_all, dtype=jnp.int32)
    gates = jnp.sum(
        probs[:, None, :]
        * (expert_ids[:, :, None] == expert_iota[None, None, :]).astype(jnp.float32),
        axis=-1,
    )
    picks = expert_ids.reshape(-1)
    pick_count = picks.shape[0]
    onehot = (picks[:, None] == expert_iota[None, :]).astype(jnp.int32)
    earlier = jnp.cumsum(onehot, axis=0) - onehot
    rank = jnp.sum(earlier * onehot, axis=1)
    slot_of_pick = picks * CAP + rank
    source = (
        jnp.full((experts_all * CAP,), tok_rows, jnp.int32)
        .at[slot_of_pick]
        .set(jnp.arange(pick_count, dtype=jnp.int32) // TOPK)
    )
    padded = jnp.concatenate([ffn_in, jnp.zeros((1, ffn_in.shape[1]), jnp.bfloat16)], axis=0)
    outgoing = jnp.take(padded, source, axis=0).reshape(
        req_size, expert_local, CAP, padded.shape[1]
    )
    served = expert_block(
        lax.all_to_all(outgoing, "req", split_axis=0, concat_axis=0, tiled=True),
        w_exp_in,
        w_exp_down,
    )
    shared_both = jnp.einsum("td,cdf->ctf", ffn_in, w_sh_in, preferred_element_type=jnp.float32)
    shared_inner = (jax.nn.silu(shared_both[0]) * shared_both[1]).astype(jnp.bfloat16)
    shared_terms = jnp.dot(shared_inner, w_sh_down, preferred_element_type=jnp.float32)
    pick_slots = slot_of_pick.reshape(tok_rows, TOPK)
    returned = lax.all_to_all(served, "req", split_axis=0, concat_axis=0, tiled=True)
    returned = returned.reshape(experts_all * CAP, returned.shape[3])
    to_reduce = shared_terms
    for pick_pos in range(TOPK):
        chosen_rows = jnp.take(returned, pick_slots[:, pick_pos], axis=0).astype(jnp.float32)
        to_reduce = to_reduce + chosen_rows * gates[:, pick_pos : pick_pos + 1]
    layer_share = lax.psum_scatter(
        to_reduce.astype(jnp.bfloat16), "tp", scatter_dimension=1, tiled=True
    ).astype(jnp.float32)
    resid_share = lax.dynamic_slice_in_dim(resid, tp_pos * local_feat, local_feat, 1)
    out_hidden = (resid_share.astype(jnp.float32) + layer_share).astype(jnp.bfloat16)
    last_share = out_hidden.reshape(slot_count, new_len, local_feat)[:, new_len - 1]
    last_rows = lax.all_gather(last_share, "tp", axis=1, tiled=True)
    last_every = lax.all_gather(last_rows, "req", axis=0, tiled=True)
    last_tok = last_every.astype(jnp.float32)
    last_rms = jnp.sqrt(jnp.mean(last_tok * last_tok, axis=-1) + epsilon)
    head_in = (last_tok / last_rms[:, None] * final_gain.astype(jnp.float32)).astype(jnp.bfloat16)
    logits = lax.dot_general(
        head_in, w_head, (((1,), (1,)), ((), ())), preferred_element_type=jnp.float32
    )
    top_logit = lax.pmax(jnp.max(logits, axis=1), ("req", "tp"))
    return (out_hidden, new_cache, last_rms, top_logit)


def solution(mesh):
    return jax.shard_map(
        local,
        mesh=mesh,
        in_specs=(
            P("req", "tp"),
            P(),
            P(None, None, "tp"),
            P("tp", None),
            P(None, "req", None, "tp"),
            P(),
            P("req"),
            P(),
            P(),
            P("req", None),
            P("req", None, None, "tp"),
            P("req", "tp", None),
            P(None, None, "tp"),
            P("tp", None),
            P(),
            P(("req", "tp"), None),
        ),
        out_specs=(P("req", "tp"), P(None, "req", None, "tp"), P(), P()),
        check_vma=False,
    )
```

profile of v0, /device:TPU:1, one launch (start us, length us, event | category | flops | bytes accessed | tf_op | source)
XLA Modules:
  0.0 697.8 jit_solution(8037834648569727721)
XLA Ops:
  7.2 3.5 copy.92
  10.7 14.8 %all-to-all-start = ((bf16[2,1,1024,256]{3,0,1,2:T(2,128)(2,1)}), bf16[2,1,1024,256]{3,0,1,2:T(2,128)(2,1)}, u32[]{:S(2)}, u32[]{:S(2)}) async-start(bf16[2,1,1024,256]{3,0,1,2:T(2,128)(2,1)} %copy.92), calls=%async_computation | async-start | bytes 2097152 | tf_op jit(solution)/shard_map/all_to_all | solution.py:99
  25.9 1.7 reduce-window.6
  28.2 32.7 %all_gather.9 = bf16[128,2048]{1,0:T(8,128)(2,1)S(1)} all-gather(bf16[128,256]{1,0:T(8,128)(2,1)S(1)} %copy-done.8), channel_id=1, replica_groups=mesh['req'=32,'tp'=8] {'tp'}, dimensions={1}, use_global_device_ids=true | all-gather | bytes 589824 | tf_op jit(solution)/shard_map/all_gather | solution.py:83
  61.7 1.4 convolution_bitcast_fusion
  63.1 2.4 copy.93
  65.5 2.8 gather_fusion
  68.3 2.4 select_bitcast_fusion
  70.7 11.3 %all-to-all-start.1 = ((bf16[2,32,32,256]{3,2,0,1:T(8,128)(2,1)}), bf16[2,32,32,256]{3,2,0,1:T(8,128)(2,1)}, u32[]{:S(2)}, u32[]{:S(2)}) async-start(bf16[2,32,32,256]{3,2,0,1:T(8,128)(2,1)} %select_bitcast_fusion), calls=%async_computation.1 | async-start | bytes 2097152 | tf_op jit(solution)/shard_map/all_to_all | solution.py:101
  83.4 0.9 slice.189
  84.3 1.6 fusion.76
  86.8 1.0 squeeze.45
  89.8 15.1 %all-to-all-done.1 = bf16[2,32,32,256]{3,2,0,1:T(8,128)(2,1)} async-done(((bf16[2,32,32,256]{3,2,0,1:T(8,128)(2,1)}), bf16[2,32,32,256]{3,2,0,1:T(8,128)(2,1)}, u32[]{:S(2)}, u32[]{:S(2)}) %all-to-all-start.1) | async-done | bytes 1048608 | tf_op jit(solution)/shard_map/all_to_all | solution.py:101
  104.9 2.3 fusion.75
  107.2 2.0 squeeze.44
  109.2 1.9 copy.100
  111.1 2.0 squeeze.42
  113.1 2.0 copy.94
  115.1 3.3 fusion.79
  118.5 1.9 convolution_convert_fusion.1
  120.4 1.1 convolution_convert_fusion
  121.6 3.5 scatter_custom_fusion
  125.2 67.9 %all-reduce.3.cloned.1.call-done = bf16[128,2048]{1,0:T(8,128)(2,1)} async-done(((bf16[128,2048]{1,0:T(8,128)(2,1)}), bf16[128,2048]{1,0:T(8,128)(2,1)}) %all-reduce.3.cloned.1.call-update) | async-done | bytes 524304 | tf_op jit(solution)/shard_map/psum | solution.py:106
  193.2 1.5 fusion.17
  195.7 0.9 copy-done.2
  197.4 10.0 %gather_fusion.1 = bf16[1024,2048]{1,0:T(8,128)(2,1)} fusion(bf16[129,2048]{1,0:T(8,128)(2,1)} %concatenate.47, s32[1024]{0:T(1024)S(1)} %fusion.61), kind=kCustom, calls=%fused_computation.7 | custom fusion | bytes 8392704 | tf_op jit(solution)/shard_map/jit(_take)/gather | solution.py:132
  207.4 2.6 broadcast_select_fusion
  210.0 106.0 %all_to_all.31 = bf16[32,1,32,2048]{3,2,1,0:T(8,128)(2,1)S(1)} all-to-all(bf16[32,1,32,2048]{3,2,1,0:T(8,128)(2,1)S(1)} %broadcast_select_fusion), channel_id=1, replica_groups=mesh['req'=32,'tp'=8] {'req'}, dimensions={0} | all-to-all | bytes 8388608 | tf_op jit(solution)/shard_map/all_to_all | solution.py:136
  316.0 2.3 fusion.13
  318.4 3.3 convert_bitcast_fusion
  321.7 6.9 all-to-all-start.3
  329.1 1.3 fusion.80
  330.6 1.9 fusion.81
  332.5 81.5 %all-to-all-done.3 = bf16[32,1,32,2048]{3,2,1,0:T(8,128)(2,1)} async-done(((bf16[32,1,32,2048]{3,2,1,0:T(8,128)(2,1)}), bf16[32,1,32,2048]{3,2,1,0:T(8,128)(2,1)}, u32[]{:S(2)}, u32[]{:S(2)}) %all-to-all-start.3) | async-done | bytes 4194336 | tf_op jit(solution)/shard_map/all_to_all | solution.py:144
  413.9 5.0 gather_fusion.7
  418.9 5.0 gather_fusion.6
  423.9 5.0 gather_fusion.5
  428.9 5.0 gather_fusion.4
  433.8 5.0 gather_fusion.3
  438.8 5.0 gather_fusion.2
  443.8 4.0 fusion.12
  448.0 0.9 slice_bitcast_fusion.8
  448.9 39.4 %reduce-scatter.2.cloned.1.call-done = bf16[128,256]{1,0:T(8,128)(2,1)} async-done(((bf16[128,2048]{1,0:T(8,128)(2,1)}), bf16[128,256]{1,0:T(8,128)(2,1)}) %reduce-scatter.2.cloned.1.call-update) | async-done | bytes 65552 | tf_op jit(solution)/shard_map/reduce_scatter | solution.py:150
  488.3 0.9 add_convert_fusion
  489.2 12.1 %all-gather = bf16[1,1,2048]{2,1,0:T(2,128)(2,1)S(1)} all-gather(bf16[1,1,256]{2,1,0:T(2,128)(2,1)S(1)} %slice.154), channel_id=2, replica_groups=mesh['req'=32,'tp'=8] {'tp'}, dimensions={2}, use_global_device_ids=true | all-gather | bytes 4608 | tf_op jit(solution)/shard_map/all_gather | solution.py:156
  501.3 101.8 %all-gather.1 = bf16[32,1,2048]{2,1,0:T(2,128)(2,1)S(1)} all-gather(bf16[1,1,2048]{2,1,0:T(2,128)(2,1)S(1)} %all-gather), channel_id=3, replica_groups=mesh['req'=32,'tp'=8] {'req'}, dimensions={0}, use_global_device_ids=true | all-gather | bytes 135168 | tf_op jit(solution)/shard_map/all_gather | solution.py:157
  603.6 1.6 convolution_reduce_fusion
  605.9 85.0 %pmax.7 = f32[32]{0:T(128)} all-reduce(f32[32]{0:T(128)S(1)} %convolution_reduce_fusion), channel_id=1, replica_groups=mesh['req'=32,'tp'=8] {'req','tp'}, use_global_device_ids=true, to_apply=%region_15.17 | all-reduce | flops 32 | bytes 256 | tf_op jit(solution)/shard_map/pmax | solution.py:164
  (101 shorter events, 9.2 us)
Async XLA Ops:
  7.2 54.5 %copy-start = (bf16[3,2048,256]{2,1,0:T(8,128)(2,1)S(1)}, bf16[3,2048,256]{2,1,0:T(8,128)(2,1)}, u32[]{:S(2)}) copy-start(bf16[3,2048,256]{2,1,0:T(8,128)(2,1)} %param.20) | copy-start | bytes 9437188
  10.7 14.8 %copy-start.10 = (s32[128,6]{0,1:T(8,128)S(1)}, s32[128,6]{0,1:T(8,128)}, u32[]{:S(2)}) copy-start(s32[128,6]{0,1:T(8,128)} %param.27) | copy-start | bytes 9220
  10.7 15.2 %copy-start.12 = (bf16[2048]{0:T(1024)(128)(2,1)S(1)}, bf16[2048]{0:T(1024)(128)(2,1)}, u32[]{:S(2)}) copy-start(bf16[2048]{0:T(1024)(128)(2,1)} %param.19) | copy-start | bytes 12292
  10.7 17.5 %copy-start.17 = (s32[32]{0:T(128)S(1)}, s32[32]{0:T(128)}, u32[]{:S(2)}) copy-start(s32[32]{0:T(128)} %param.23) | copy-start | bytes 388
  10.7 17.5 %copy-start.8 = (bf16[128,256]{1,0:T(8,128)(2,1)S(1)}, bf16[128,256]{1,0:T(8,128)(2,1)}, u32[]{:S(2)}) copy-start(bf16[128,256]{1,0:T(8,128)(2,1)} %param.18) | copy-start | bytes 196612
  10.7 52.4 %all-to-all-start = ((bf16[2,1,1024,256]{3,0,1,2:T(2,128)(2,1)}), bf16[2,1,1024,256]{3,0,1,2:T(2,128)(2,1)}, u32[]{:S(2)}, u32[]{:S(2)}) async-start(bf16[2,1,1024,256]{3,0,1,2:T(2,128)(2,1)} %copy.92), calls=%async_computation | async-start | bytes 2097152 | tf_op jit(solution)/shard_map/all_to_all | solution.py:99
  60.9 0.8 copy-start.1
  70.7 12.0 %copy-start.13 = (bf16[2048]{0:T(1024)(128)(2,1)S(1)}, bf16[2048]{0:T(1024)(128)(2,1)}, u32[]{:S(2)}) copy-start(bf16[2048]{0:T(1024)(128)(2,1)} %param.25) | copy-start | bytes 12292
  70.7 34.3 %all-to-all-start.1 = ((bf16[2,32,32,256]{3,2,0,1:T(8,128)(2,1)}), bf16[2,32,32,256]{3,2,0,1:T(8,128)(2,1)}, u32[]{:S(2)}, u32[]{:S(2)}) async-start(bf16[2,32,32,256]{3,2,0,1:T(8,128)(2,1)} %select_bitcast_fusion), calls=%async_computation.1 | async-start | bytes 2097152 | tf_op jit(solution)/shard_map/all_to_all | solution.py:101
  81.9 111.3 %all-reduce.3.cloned.1.call-start = ((), (), s32[]{:S(2)}) async-start(), calls=%async_computation.5 | async-start | bytes 1048576 | tf_op jit(solution)/shard_map/psum | solution.py:106
  118.5 2.0 copy-start.5
  121.6 73.9 %copy-start.9 = (f32[2048]{0:T(1024)S(1)}, f32[2048]{0:T(1024)}, u32[]{:S(2)}) copy-start(f32[2048]{0:T(1024)} %convert_element_type.185) | copy-start | bytes 24580
  194.6 0.8 copy-start.4
  195.7 0.9 copy-start.2
  210.0 106.0 %copy-start.15 = (bf16[1,2,2048,176]{2,3,1,0:T(8,128)(2,1)S(1)}, bf16[1,2,2048,176]{2,3,1,0:T(8,128)(2,1)}, u32[]{:S(2)}) copy-start(bf16[1,2,2048,176]{2,3,1,0:T(8,128)(2,1)} %param.28) | copy-start | bytes 4325380
  316.0 2.3 copy-start.16
  321.7 7.4 %copy-start.6 = (bf16[2048,32]{0,1:T(8,128)(2,1)S(1)}, bf16[2048,32]{0,1:T(8,128)(2,1)}, u32[]{:S(2)}) copy-start(bf16[2048,32]{0,1:T(8,128)(2,1)} %param.26) | copy-start | bytes 393220
  321.7 8.8 %copy-start.11 = (s32[128,6]{0,1:T(8,128)S(1)}, s32[128,6]{0,1:T(8,128)}, u32[]{:S(2)}) copy-start(s32[128,6]{0,1:T(8,128)} %param.27) | copy-start | bytes 9220
  321.7 92.3 %all-to-all-start.3 = ((bf16[32,1,32,2048]{3,2,1,0:T(8,128)(2,1)}), bf16[32,1,32,2048]{3,2,1,0:T(8,128)(2,1)}, u32[]{:S(2)}, u32[]{:S(2)}) async-start(bf16[32,1,32,2048]{3,2,1,0:T(8,128)(2,1)} %convert_bitcast_fusion), calls=%async_computation.3 | async-start | bytes 8388608 | tf_op jit(solution)/shard_map/all_to_all | solution.py:144
  328.6 159.7 %reduce-scatter.2.cloned.1.call-start = ((), (), s32[]{:S(2)}) async-start(), calls=%async_computation.6 | async-start | bytes 589824 | tf_op jit(solution)/shard_map/reduce_scatter | solution.py:150
  328.6 1.9 copy-start.3
  443.8 4.1 copy-start.14
  489.2 116.8 %copy-start.7 = (bf16[128,256]{1,0:T(8,128)(2,1)}, bf16[128,256]{1,0:T(8,128)(2,1)S(1)}, u32[]{:S(2)}) copy-start(bf16[128,256]{1,0:T(8,128)(2,1)S(1)} %add_convert_fusion) | copy-start | bytes 196612
  603.6 87.3 %copy-start.18 = (f32[32]{0:T(128)}, f32[32]{0:T(128)S(1)}, u32[]{:S(2)}) copy-start(f32[32]{0:T(128)S(1)} %add_sqrt_fusion) | copy-start | bytes 388
Sparse Core Ops, SparseCore 0:
  121.7 71.4 all-reduce.2
  448.0 40.2 reduce-scatter.1
where the time goes:
time: 699 us; the launch traced here: 698 us
  blocking collectives  338 us (48%)
  waiting for transfers between devices  204 us (29%)
  local copies, waits for them, and re-layouts  72.3 us (10%)
  starting transfers between devices  33 us (5%)
  matrix products  22.3 us (3%)
  between operations  15.2 us (2%)
  other arithmetic  13.4 us (2%)
    all_to_all x1, blocking collectives, local(): lax.all_to_all(outgoing, 'req', split_axis=0, concat_axis=0, tiled=True)  106 us
    all_gather x1, blocking collectives, local(): last_every = lax.all_gather(last_rows, 'req', axis=0, tiled=True)  102 us
    pmax x1, blocking collectives, local(): top_logit = lax.pmax(jnp.max(logits, axis=1), ('req', 'tp'))  85 us
    all_to_all x1, waiting for transfers between devices, local(): lax.all_to_all(served, 'req', split_axis=0, concat_axis=0, tiled=True)  81.5 us
    psum x1, waiting for transfers between devices, local(): lax.psum(jnp.dot(attn_out, w_out, preferred_element_type=jnp.float32).ast...  67.9 us
    reduce_scatter x1, waiting for transfers between devices, local(): lax.psum_scatter(to_reduce.astype(jnp.bfloat16), 'tp', scatter_dimension=...  39.4 us
    all_gather x1, blocking collectives, local(): full_in = lax.all_gather(hidden, 'tp', axis=1, tiled=True)  32.7 us
    gather x6, local copies, waits for them, and re-layouts, local(): jnp.take(returned, pick_slots[:, pick_pos], axis=0).astype(jnp.float32)  29.9 us
  transfers between devices with their start and end apart: 5, of which 4 were waited for; matrix products, arithmetic and copies ran while one was open for 3% of the time, Pallas kernels for 0%

commit v1 on v0

--- a/solution.py
+++ b/solution.py
@@ -80,7 +80,8 @@
 ):
     req_size = lax.axis_size("req")
     tp_pos = lax.axis_index("tp")
-    full_in = lax.all_gather(hidden, "tp", axis=1, tiled=True)
+    stack = jnp.stack([hidden] * lax.axis_size("tp"))
+    full_in = jnp.concatenate(lax.all_to_all(stack, "tp", 0, 0), axis=1)
     tok_rows = full_in.shape[0]
     slot_count = kv_cache.shape[1]
     new_len = tok_rows // slot_count

time: 699 us -> 698 us (level)
  blocking collectives: 338 us -> 305 us
  waiting for transfers between devices: 204 us -> 224 us
  starting transfers between devices: 33 us -> 40.4 us
    all_gather x1 -> x0, blocking collectives: 32.7 us -> none  [local(): full_in = lax.all_gather(hidden, 'tp', axis=1, tiled=True)]
    all_to_all x1, waiting for transfers between devices: 0.01 us -> 16.2 us  [local(): lax.all_to_all(kv_cache, 'req', split_axis=2, concat_axis=1, tiled=True)]
    all_to_all x0 -> x1, starting transfers between devices: none -> 14 us  [local(): full_in = jnp.concatenate(lax.all_to_all(stack, 'tp', 0, 0), axis=1)]
  transfers between devices with their start and end apart: 5 -> 6, of which waited for: 4 -> 6; matrix products, arithmetic and copies ran while one was open for 3% -> 4% of each run, Pallas kernels for 0% -> 0%
where the time goes in v1:
time: 698 us; the launch traced here: 697 us
  blocking collectives  305 us (44%)
  waiting for transfers between devices  224 us (32%)
  local copies, waits for them, and re-layouts  72.3 us (10%)
  starting transfers between devices  40.4 us (6%)
  matrix products  21.6 us (3%)
  other arithmetic  18.2 us (3%)
  between operations  15.3 us (2%)
    all_to_all x1, blocking collectives, local(): lax.all_to_all(outgoing, 'req', split_axis=0, concat_axis=0, tiled=True)  106 us
    all_gather x1, blocking collectives, local(): last_every = lax.all_gather(last_rows, 'req', axis=0, tiled=True)  102 us
    pmax x1, blocking collectives, local(): top_logit = lax.pmax(jnp.max(logits, axis=1), ('req', 'tp'))  84.9 us
    all_to_all x1, waiting for transfers between devices, local(): lax.all_to_all(served, 'req', split_axis=0, concat_axis=0, tiled=True)  81.4 us
    psum x1, waiting for transfers between devices, local(): lax.psum(jnp.dot(attn_out, w_out, preferred_element_type=jnp.float32).ast...  64 us
    reduce_scatter x1, waiting for transfers between devices, local(): lax.psum_scatter(to_reduce.astype(jnp.bfloat16), 'tp', scatter_dimension=...  39.4 us
    gather x6, local copies, waits for them, and re-layouts, local(): jnp.take(returned, pick_slots[:, pick_pos], axis=0).astype(jnp.float32)  29.9 us
    all_to_all x1, waiting for transfers between devices, local(): lax.all_to_all(ordered, 'req', split_axis=1, concat_axis=2, tiled=True)  16.5 us
  transfers between devices with their start and end apart: 6, of which 6 were waited for; matrix products, arithmetic and copies ran while one was open for 4% of the time, Pallas kernels for 0%

profile of v1, /device:TPU:1, one launch (start us, length us, event | category | flops | bytes accessed | tf_op | source)
XLA Modules:
  0.0 696.6 jit_solution(441520342853747126)
XLA Ops:
  7.2 3.5 copy.95
  10.7 14.8 %all-to-all-start.1 = ((bf16[2,1,1024,256]{3,0,1,2:T(2,128)(2,1)}), bf16[2,1,1024,256]{3,0,1,2:T(2,128)(2,1)}, u32[]{:S(2)}, u32[]{:S(2)}) async-start(bf16[2,1,1024,256]{3,0,1,2:T(2,128)(2,1)} %copy.95), calls=%async_computation.1 | async-start | bytes 2097152 | tf_op jit(solution)/shard_map/all_to_all | solution.py:100
  27.2 1.7 reduce-window.6
  30.3 16.2 %all-to-all-done.1 = bf16[2,1,1024,256]{3,0,1,2:T(2,128)(2,1)} async-done(((bf16[2,1,1024,256]{3,0,1,2:T(2,128)(2,1)}), bf16[2,1,1024,256]{3,0,1,2:T(2,128)(2,1)}, u32[]{:S(2)}, u32[]{:S(2)}) %all-to-all-start.1) | async-done | bytes 1048608 | tf_op jit(solution)/shard_map/all_to_all | solution.py:100
  47.3 14.0 %all-to-all-start = ((bf16[8,128,256]{2,1,0:T(8,128)(2,1)}), bf16[8,128,256]{2,1,0:T(8,128)(2,1)}, u32[]{:S(2)}, u32[]{:S(2)}) async-start(bf16[8,128,256]{2,1,0:T(8,128)(2,1)} %stack.4), calls=%async_computation | async-start | bytes 1048576 | tf_op jit(solution)/shard_map/all_to_all | solution.py:84
  62.1 2.4 copy.96
  64.5 2.8 gather_fusion
  67.4 2.4 select_bitcast_fusion
  69.7 6.2 all-to-all-done
  76.0 4.7 all-to-all-start.2
  81.6 1.1 convert_bitcast_fusion.1
  82.9 1.6 fusion.20
  86.7 1.6 copy.112
  88.2 1.0 squeeze.45
  89.6 1.6 fusion.48
  91.1 16.5 %all-to-all-done.2 = bf16[2,32,32,256]{3,2,0,1:T(8,128)(2,1)} async-done(((bf16[2,32,32,256]{3,2,0,1:T(8,128)(2,1)}), bf16[2,32,32,256]{3,2,0,1:T(8,128)(2,1)}, u32[]{:S(2)}, u32[]{:S(2)}) %all-to-all-start.2) | async-done | bytes 1048608 | tf_op jit(solution)/shard_map/all_to_all | solution.py:102
  107.7 2.3 fusion.71
  109.9 2.0 squeeze.44
  111.9 1.9 copy.103
  113.8 2.0 squeeze.42
  115.8 2.0 copy.97
  117.8 3.4 fusion.75
  121.2 1.9 convolution_convert_fusion.1
  123.2 1.1 convolution_convert_fusion
  124.4 3.5 scatter_custom_fusion
  128.0 64.0 %all-reduce.3.cloned.1.call-done = bf16[128,2048]{1,0:T(8,128)(2,1)} async-done(((bf16[128,2048]{1,0:T(8,128)(2,1)}), bf16[128,2048]{1,0:T(8,128)(2,1)}) %all-reduce.3.cloned.1.call-update) | async-done | bytes 524304 | tf_op jit(solution)/shard_map/psum | solution.py:107
  192.0 1.6 fusion.17
  196.3 10.0 %gather_fusion.1 = bf16[1024,2048]{1,0:T(8,128)(2,1)} fusion(bf16[129,2048]{1,0:T(8,128)(2,1)} %concatenate.47, s32[1024]{0:T(1024)S(1)} %fusion.58), kind=kCustom, calls=%fused_computation.7 | custom fusion | bytes 8392704 | tf_op jit(solution)/shard_map/jit(_take)/gather | solution.py:133
  206.3 2.6 broadcast_select_fusion
  208.9 106.0 %all_to_all.36 = bf16[32,1,32,2048]{3,2,1,0:T(8,128)(2,1)S(1)} all-to-all(bf16[32,1,32,2048]{3,2,1,0:T(8,128)(2,1)S(1)} %broadcast_select_fusion), channel_id=1, replica_groups=mesh['req'=32,'tp'=8] {'req'}, dimensions={0} | all-to-all | bytes 8388608 | tf_op jit(solution)/shard_map/all_to_all | solution.py:137
  314.9 2.3 fusion.13
  317.3 3.3 convert_bitcast_fusion
  320.6 6.9 all-to-all-start.4
  328.0 1.3 fusion.76
  329.5 1.9 fusion.77
  331.4 81.4 %all-to-all-done.4 = bf16[32,1,32,2048]{3,2,1,0:T(8,128)(2,1)} async-done(((bf16[32,1,32,2048]{3,2,1,0:T(8,128)(2,1)}), bf16[32,1,32,2048]{3,2,1,0:T(8,128)(2,1)}, u32[]{:S(2)}, u32[]{:S(2)}) %all-to-all-start.4) | async-done | bytes 4194336 | tf_op jit(solution)/shard_map/all_to_all | solution.py:145
  412.8 5.0 gather_fusion.7
  417.8 5.0 gather_fusion.6
  422.7 5.0 gather_fusion.5
  427.7 5.0 gather_fusion.4
  432.7 5.0 gather_fusion.3
  437.7 5.0 gather_fusion.2
  442.6 4.0 fusion.12
  447.7 39.4 %reduce-scatter.2.cloned.1.call-done = bf16[128,256]{1,0:T(8,128)(2,1)} async-done(((bf16[128,2048]{1,0:T(8,128)(2,1)}), bf16[128,256]{1,0:T(8,128)(2,1)}) %reduce-scatter.2.cloned.1.call-update) | async-done | bytes 65552 | tf_op jit(solution)/shard_map/reduce_scatter | solution.py:151
  488.0 12.2 %all-gather = bf16[1,1,2048]{2,1,0:T(2,128)(2,1)S(1)} all-gather(bf16[1,1,256]{2,1,0:T(2,128)(2,1)S(1)} %slice.154), channel_id=2, replica_groups=mesh['req'=32,'tp'=8] {'tp'}, dimensions={2}, use_global_device_ids=true | all-gather | bytes 4608 | tf_op jit(solution)/shard_map/all_gather | solution.py:157
  500.2 101.9 %all-gather.1 = bf16[32,1,2048]{2,1,0:T(2,128)(2,1)S(1)} all-gather(bf16[1,1,2048]{2,1,0:T(2,128)(2,1)S(1)} %all-gather), channel_id=3, replica_groups=mesh['req'=32,'tp'=8] {'req'}, dimensions={0}, use_global_device_ids=true | all-gather | bytes 135168 | tf_op jit(solution)/shard_map/all_gather | solution.py:158
  602.5 1.6 convolution_reduce_fusion
  604.8 84.9 %pmax.7 = f32[32]{0:T(128)} all-reduce(f32[32]{0:T(128)S(1)} %convolution_reduce_fusion), channel_id=1, replica_groups=mesh['req'=32,'tp'=8] {'req','tp'}, use_global_device_ids=true, to_apply=%region_15.17 | all-reduce | flops 32 | bytes 256 | tf_op jit(solution)/shard_map/pmax | solution.py:165
  (111 shorter events, 13.9 us)
Async XLA Ops:
  7.2 77.3 %copy-start = (bf16[3,2048,256]{2,1,0:T(8,128)(2,1)S(1)}, bf16[3,2048,256]{2,1,0:T(8,128)(2,1)}, u32[]{:S(2)}) copy-start(bf16[3,2048,256]{2,1,0:T(8,128)(2,1)} %param.20) | copy-start | bytes 9437188
  10.7 14.8 %copy-start.13 = (s32[128,6]{0,1:T(8,128)S(1)}, s32[128,6]{0,1:T(8,128)}, u32[]{:S(2)}) copy-start(s32[128,6]{0,1:T(8,128)} %param.27) | copy-start | bytes 9220
  10.7 15.9 %copy-start.15 = (bf16[2048]{0:T(1024)(128)(2,1)S(1)}, bf16[2048]{0:T(1024)(128)(2,1)}, u32[]{:S(2)}) copy-start(bf16[2048]{0:T(1024)(128)(2,1)} %param.19) | copy-start | bytes 12292
  10.7 15.9 %copy-start.16 = (bf16[2048]{0:T(1024)(128)(2,1)S(1)}, bf16[2048]{0:T(1024)(128)(2,1)}, u32[]{:S(2)}) copy-start(bf16[2048]{0:T(1024)(128)(2,1)} %param.25) | copy-start | bytes 12292
  10.7 19.0 %copy-start.20 = (s32[32]{0:T(128)S(1)}, s32[32]{0:T(128)}, u32[]{:S(2)}) copy-start(s32[32]{0:T(128)} %param.23) | copy-start | bytes 388
  10.7 35.8 %copy-start.11 = (bf16[128,256]{1,0:T(8,128)(2,1)S(1)}, bf16[128,256]{1,0:T(8,128)(2,1)}, u32[]{:S(2)}) copy-start(bf16[128,256]{1,0:T(8,128)(2,1)} %param.18) | copy-start | bytes 196612
  10.7 35.8 %all-to-all-start.1 = ((bf16[2,1,1024,256]{3,0,1,2:T(2,128)(2,1)}), bf16[2,1,1024,256]{3,0,1,2:T(2,128)(2,1)}, u32[]{:S(2)}, u32[]{:S(2)}) async-start(bf16[2,1,1024,256]{3,0,1,2:T(2,128)(2,1)} %copy.95), calls=%async_computation.1 | async-start | bytes 2097152 | tf_op jit(solution)/shard_map/all_to_all | solution.py:100
  47.3 28.6 %all-to-all-start = ((bf16[8,128,256]{2,1,0:T(8,128)(2,1)}), bf16[8,128,256]{2,1,0:T(8,128)(2,1)}, u32[]{:S(2)}, u32[]{:S(2)}) async-start(bf16[8,128,256]{2,1,0:T(8,128)(2,1)} %stack.4), calls=%async_computation | async-start | bytes 1048576 | tf_op jit(solution)/shard_map/all_to_all | solution.py:84
  76.0 31.7 %all-to-all-start.2 = ((bf16[2,32,32,256]{3,2,0,1:T(8,128)(2,1)}), bf16[2,32,32,256]{3,2,0,1:T(8,128)(2,1)}, u32[]{:S(2)}, u32[]{:S(2)}) async-start(bf16[2,32,32,256]{3,2,0,1:T(8,128)(2,1)} %select_bitcast_fusion), calls=%async_computation.2 | async-start | bytes 2097152 | tf_op jit(solution)/shard_map/all_to_all | solution.py:102
  80.6 111.3 %all-reduce.3.cloned.1.call-start = ((), (), s32[]{:S(2)}) async-start(), calls=%async_computation.6 | async-start | bytes 1048576 | tf_op jit(solution)/shard_map/psum | solution.py:107
  82.9 2.3 copy-start.1
  85.2 0.8 copy-start.5
  111.9 5.9 copy-start.7
  111.9 5.9 copy-start.10
  121.2 2.0 copy-start.6
  124.3 70.1 %copy-start.12 = (f32[2048]{0:T(1024)S(1)}, f32[2048]{0:T(1024)}, u32[]{:S(2)}) copy-start(f32[2048]{0:T(1024)} %convert_element_type.198) | copy-start | bytes 24580
  193.6 0.8 copy-start.4
  194.6 0.9 copy-start.2
  208.9 106.0 %copy-start.18 = (bf16[1,2,2048,176]{2,3,1,0:T(8,128)(2,1)S(1)}, bf16[1,2,2048,176]{2,3,1,0:T(8,128)(2,1)}, u32[]{:S(2)}) copy-start(bf16[1,2,2048,176]{2,3,1,0:T(8,128)(2,1)} %param.28) | copy-start | bytes 4325380
  314.9 2.3 copy-start.19
  320.6 7.4 %copy-start.8 = (bf16[2048,32]{0,1:T(8,128)(2,1)S(1)}, bf16[2048,32]{0,1:T(8,128)(2,1)}, u32[]{:S(2)}) copy-start(bf16[2048,32]{0,1:T(8,128)(2,1)} %param.26) | copy-start | bytes 393220
  320.6 8.8 %copy-start.14 = (s32[128,6]{0,1:T(8,128)S(1)}, s32[128,6]{0,1:T(8,128)}, u32[]{:S(2)}) copy-start(s32[128,6]{0,1:T(8,128)} %param.27) | copy-start | bytes 9220
  320.6 92.2 %all-to-all-start.4 = ((bf16[32,1,32,2048]{3,2,1,0:T(8,128)(2,1)}), bf16[32,1,32,2048]{3,2,1,0:T(8,128)(2,1)}, u32[]{:S(2)}, u32[]{:S(2)}) async-start(bf16[32,1,32,2048]{3,2,1,0:T(8,128)(2,1)} %convert_bitcast_fusion), calls=%async_computation.4 | async-start | bytes 8388608 | tf_op jit(solution)/shard_map/all_to_all | solution.py:145
  327.5 159.6 %reduce-scatter.2.cloned.1.call-start = ((), (), s32[]{:S(2)}) async-start(), calls=%async_computation.7 | async-start | bytes 589824 | tf_op jit(solution)/shard_map/reduce_scatter | solution.py:151
  327.5 1.9 copy-start.3
  442.6 4.1 copy-start.17
  488.0 116.8 %copy-start.9 = (bf16[128,256]{1,0:T(8,128)(2,1)}, bf16[128,256]{1,0:T(8,128)(2,1)S(1)}, u32[]{:S(2)}) copy-start(bf16[128,256]{1,0:T(8,128)(2,1)S(1)} %add_convert_fusion.1) | copy-start | bytes 196612
  602.5 87.3 %copy-start.21 = (f32[32]{0:T(128)}, f32[32]{0:T(128)S(1)}, u32[]{:S(2)}) copy-start(f32[32]{0:T(128)S(1)} %add_sqrt_fusion) | copy-start | bytes 388
Sparse Core Ops, SparseCore 0:
  124.5 67.4 all-reduce.2
  446.8 40.2 reduce-scatter.1
